TPU v7x, 32 devices: a whole 2x2x4 slice. The times are simulated.
32 devices in a mesh: group: 4 (over y, core), member: 8 (over z, x).
Axes of the slice: x: 2, y: 2, z: 4, core: 2. Of those that a mesh axis runs over, the one named last changes fastest.
Arguments:
- features: bfloat16 [16384, 128], P(('group', 'member')), may hold values from -6 to 6
- edge_tiles: bfloat16 [8192, 128, 128], P(('group', 'member')), may hold values from -0.09375 to 0.09375
- tile_slot: int32 [32, 256], P(('group', 'member')), may hold values from 0 to 7
- tile_column: int32 [32, 256], P(('group', 'member')), may hold values from 0 to 31
- mirror_count: int32 [32, 4], P(('group', 'member')), may hold values from 0 to 2, as said below
- mirror_block: int32 [32, 4, 2], P(('group', 'member')), may hold values from 0 to 3, as said below
- weight_first: bfloat16 [128, 256], replicated, may hold values from -0.5 to 0.5
- bias_first: float32 [256], replicated, may hold values from -3 to 3
- weight_second: bfloat16 [256, 256], replicated, may hold values from -0.375 to 0.375
- bias_second: float32 [256], replicated, may hold values from -3 to 3
Outputs:
- layer_out: bfloat16 [16384, 256], P(('group', 'member'))
Inputs may be any that keep to these rules, and one draw needn't show every extreme that they name: `mirror_count`: at most 2 live mirror slots of one device for one destination group. `mirror_block`: the 2 entries of one device and destination group are distinct.
All inputs are finite; a program needn't handle non-finite values.
Results may differ from a plain program's by a relative error of at most 0.01.
Values may be sent and summed in bfloat16 or wider, within the bound.
A program may use at most 64 MiB of HBM per device.

v0:
```python
import math
import jax
import jax.numpy as jnp
from jax import lax
from jax.sharding import PartitionSpec as P


def expand(owners, block_count):
    return (owners[..., None] == jnp.arange(block_count)[None, None, :]).astype(jnp.bfloat16)


def fold_tiles(sources, edge_tiles, slot_ids, column_ids, alive_mask, slot_total):
    tile_total = edge_tiles.shape[0]
    tile_size = edge_tiles.shape[1]
    channels = sources.shape[2]
    block_tiles = math.gcd(tile_total, 32)
    rounds = tile_total // block_tiles
    tile_sets = edge_tiles.reshape(rounds, block_tiles, tile_size, tile_size)
    slot_sets = slot_ids.reshape(rounds, block_tiles)
    column_sets = column_ids.reshape(rounds, block_tiles)
    alive_sets = alive_mask.astype(jnp.float32).reshape(rounds, block_tiles)

    def advance(totals, pieces):
        tile_set, column_set, slot_set, alive_set = pieces
        source = jnp.take(sources, column_set, axis=0)
        products = jnp.einsum("tij,tjf->tif", tile_set, source, preferred_element_type=jnp.float32)
        return (totals.at[slot_set].add(products * alive_set[:, None, None]), None)

    start = jnp.zeros((slot_total, tile_size, channels), jnp.float32)
    totals, _ = lax.scan(advance, start, (tile_sets, column_sets, slot_sets, alive_sets))
    return totals.astype(jnp.bfloat16)


def body(
    features,
    edge_tiles,
    tile_slot,
    tile_column,
    mirror_count,
    mirror_block,
    weight_first,
    bias_first,
    weight_second,
    bias_second,
):
    group_count = lax.axis_size("group")
    slot_room = mirror_block.shape[2]
    tile_size = edge_tiles.shape[1]
    block_count = features.shape[0] // tile_size
    slot_ids = tile_slot[0]
    column_ids = tile_column[0]
    counts = mirror_count[0]
    targets = mirror_block[0]
    dest_group = slot_ids // slot_room
    within = slot_ids % slot_room
    count_of = jnp.sum(
        jnp.where(dest_group[:, None] == jnp.arange(group_count)[None, :], counts[None, :], 0),
        axis=1,
    )
    alive_mask = within < count_of
    spread = expand(targets, block_count)
    slot_total = group_count * slot_room

    def reduce_rows(partials):
        channels = partials.shape[2]
        spread_sums = jnp.einsum(
            "gcb,gcif->gbif",
            spread,
            partials.reshape(group_count, slot_room, tile_size, channels),
            preferred_element_type=jnp.float32,
        )
        return lax.psum_scatter(
            spread_sums.reshape(group_count * block_count, tile_size, channels).astype(
                jnp.bfloat16
            ),
            "group",
            scatter_dimension=0,
            tiled=True,
        ).astype(jnp.float32)

    local_rows = features.reshape(block_count, tile_size, features.shape[1])
    gathered = lax.all_gather(local_rows, "member", axis=0, tiled=True)
    first_sum = reduce_rows(
        fold_tiles(gathered, edge_tiles, slot_ids, column_ids, alive_mask, slot_total)
    ).astype(jnp.bfloat16)
    flat = first_sum.reshape(-1, first_sum.shape[2])
    result = jnp.maximum(
        jnp.dot(flat, weight_first, preferred_element_type=jnp.float32) + bias_first, 0.0
    )
    hidden = result.astype(jnp.bfloat16).reshape(first_sum.shape[0], tile_size, -1)
    sources = lax.all_gather(hidden, "member", axis=0, tiled=True)
    second = reduce_rows(
        fold_tiles(sources, edge_tiles, slot_ids, column_ids, alive_mask, slot_total)
    ).astype(jnp.bfloat16)
    flat_second = second.reshape(block_count * tile_size, -1)
    return (
        jnp.dot(flat_second, weight_second, preferred_element_type=jnp.float32) + bias_second
    ).astype(jnp.bfloat16)


def solution(mesh):
    placed = (
        P(("group", "member"), None),
        P(("group", "member"), None, None),
        P(("group", "member"), None),
        P(("group", "member"), None),
        P(("group", "member"), None),
        P(("group", "member"), None, None),
        P(),
        P(),
        P(),
        P(),
    )
    return jax.shard_map(
        body, mesh=mesh, in_specs=placed, out_specs=P(("group", "member"), None), check_vma=False
    )
```

profile of v0, /device:TPU:0, one launch (start us, length us, event | category | flops | bytes accessed | tf_op | source)
XLA Modules:
  0.0 324.9 jit_solution(12725843926485415464)
XLA Ops:
  13.1 39.3 %all-gather.3.cloned.1.call-done = bf16[32,128,128]{2,1,0:T(8,128)(2,1)} async-done(((bf16[4,128,128]{2,1,0:T(8,128)(2,1)}), bf16[32,128,128]{2,1,0:T(8,128)(2,1)}) %all-gather.3.cloned.1.call-update) | async-done | bytes 1048592 | tf_op jit(solution)/shard_map/all_gather | solution.py:82
  52.4 62.0 %while.20 = (s32[]{:T(128)}, f32[8,128,128]{2,1,0:T(8,128)S(1)}, s32[8,32]{1,0:T(8,128)S(1)}, bf16[8,32,128,128]{3,2,1,0:T(8,128)(2,1)}, s32[8,32]{1,0:T(8,128)S...) while((s32[]{:T(128)}, f32[8,128,128]{2,1,0:T(8,128)S(1)}, s32[8,32]{1,0:T(8,128)S(1)}, ...), condition=%wide.region_3.4_spmd, body=%wide.region_1.3_spmd.sunk | while | flops 135792000 | bytes 12589089 | solution.py:30
  52.5 2.9 gather_fusion
  60.2 2.9 gather_fusion
  67.9 2.9 gather_fusion
  75.7 2.9 gather_fusion
  83.4 2.9 gather_fusion
  88.5 2.7 scatter_fusion
  91.2 2.9 gather_fusion
  98.9 2.9 gather_fusion
  104.0 2.7 scatter_fusion
  106.7 2.9 gather_fusion
  116.0 20.5 %reduce-scatter.3.cloned.1.call-done = bf16[4,128,128]{2,1,0:T(8,128)(2,1)} async-done(((bf16[16,128,128]{2,1,0:T(8,128)(2,1)}), bf16[4,128,128]{2,1,0:T(8,128)(2,1)}) %reduce-scatter.3.cloned.1.call-update) | async-done | bytes 131088 | tf_op jit(solution)/shard_map/reduce_scatter | solution.py:72
  138.4 49.8 %all-gather.5.cloned.1.call-done = bf16[32,128,256]{2,1,0:T(8,128)(2,1)} async-done(((bf16[4,128,256]{2,1,0:T(8,128)(2,1)}), bf16[32,128,256]{2,1,0:T(8,128)(2,1)}) %all-gather.5.cloned.1.call-update) | async-done | bytes 2097168 | tf_op jit(solution)/shard_map/all_gather | solution.py:91
  188.3 102.1 %while.21 = (s32[]{:T(128)}, f32[8,128,256]{2,1,0:T(8,128)S(1)}, s32[8,32]{1,0:T(8,128)S(1)}, bf16[8,32,128,128]{3,2,1,0:T(8,128)(2,1)}, s32[8,32]{1,0:T(8,128)S...) while((s32[]{:T(128)}, f32[8,128,256]{2,1,0:T(8,128)S(1)}, s32[8,32]{1,0:T(8,128)S(1)}, ...), condition=%wide.region_7.8_spmd, body=%wide.region_5.7_spmd.sunk | while | flops 271582592 | bytes 24123424 | solution.py:30
  190.7 3.9 %convolution_multiply_fusion.5 = f32[32,128,256]{2,1,0:T(8,128)} fusion(f32[32]{0:T(128)S(1)} %fusion.53, bf16[32,128,256]{2,1,0:T(8,128)(2,1)S(1)} %gather_fusion.1, pred[32]{0:T(512)(128)(4,1)S(1)} %compare_and_fusion.5, bf16[8,32,128,128]{3,2,1,0:T(8,128)(2,1)} %get-tuple-element.250, s32[]{:T(128)} %get-tuple-element.239), kind=kOutput, calls=%fused_computation.24.clone.1 | convolution fusion | flops 270532608 | bytes 7340704 | tf_op jit(solution)/shard_map/while/body/eval_jaxpr/tij,tjf->tif/dot_general | solution.py:26
  194.6 6.4 %scatter_fusion.1 = f32[8,128,256]{2,1,0:T(8,128)S(1)} fusion(f32[8,128,256]{2,1,0:T(8,128)S(1)} %get-tuple-element.240, s32[32]{0:T(128)S(1)} %get-tuple-element.205, f32[32,128,256]{2,1,0:T(8,128)} %convolution_multiply_fusion.5), kind=kCustom, calls=%fused_computation.3.clone.1 | custom fusion | flops 1048576 | bytes 12583040 | tf_op jit(solution)/shard_map/while/body/eval_jaxpr/scatter-add | solution.py:27
  203.4 3.9 %convolution_multiply_fusion.5 = f32[32,128,256]{2,1,0:T(8,128)} fusion(f32[32]{0:T(128)S(1)} %fusion.53, bf16[32,128,256]{2,1,0:T(8,128)(2,1)S(1)} %gather_fusion.1, pred[32]{0:T(512)(128)(4,1)S(1)} %compare_and_fusion.5, bf16[8,32,128,128]{3,2,1,0:T(8,128)(2,1)} %get-tuple-element.250, s32[]{:T(128)} %get-tuple-element.239), kind=kOutput, calls=%fused_computation.24.clone.1 | convolution fusion | flops 270532608 | bytes 7340704 | tf_op jit(solution)/shard_map/while/body/eval_jaxpr/tij,tjf->tif/dot_general | solution.py:26
  207.3 6.4 %scatter_fusion.1 = f32[8,128,256]{2,1,0:T(8,128)S(1)} fusion(f32[8,128,256]{2,1,0:T(8,128)S(1)} %get-tuple-element.240, s32[32]{0:T(128)S(1)} %get-tuple-element.205, f32[32,128,256]{2,1,0:T(8,128)} %convolution_multiply_fusion.5), kind=kCustom, calls=%fused_computation.3.clone.1 | custom fusion | flops 1048576 | bytes 12583040 | tf_op jit(solution)/shard_map/while/body/eval_jaxpr/scatter-add | solution.py:27
  216.2 3.9 %convolution_multiply_fusion.5 = f32[32,128,256]{2,1,0:T(8,128)} fusion(f32[32]{0:T(128)S(1)} %fusion.53, bf16[32,128,256]{2,1,0:T(8,128)(2,1)S(1)} %gather_fusion.1, pred[32]{0:T(512)(128)(4,1)S(1)} %compare_and_fusion.5, bf16[8,32,128,128]{3,2,1,0:T(8,128)(2,1)} %get-tuple-element.250, s32[]{:T(128)} %get-tuple-element.239), kind=kOutput, calls=%fused_computation.24.clone.1 | convolution fusion | flops 270532608 | bytes 7340704 | tf_op jit(solution)/shard_map/while/body/eval_jaxpr/tij,tjf->tif/dot_general | solution.py:26
  220.1 6.5 %scatter_fusion.1 = f32[8,128,256]{2,1,0:T(8,128)S(1)} fusion(f32[8,128,256]{2,1,0:T(8,128)S(1)} %get-tuple-element.240, s32[32]{0:T(128)S(1)} %get-tuple-element.205, f32[32,128,256]{2,1,0:T(8,128)} %convolution_multiply_fusion.5), kind=kCustom, calls=%fused_computation.3.clone.1 | custom fusion | flops 1048576 | bytes 12583040 | tf_op jit(solution)/shard_map/while/body/eval_jaxpr/scatter-add | solution.py:27
  228.9 3.9 %convolution_multiply_fusion.5 = f32[32,128,256]{2,1,0:T(8,128)} fusion(f32[32]{0:T(128)S(1)} %fusion.53, bf16[32,128,256]{2,1,0:T(8,128)(2,1)S(1)} %gather_fusion.1, pred[32]{0:T(512)(128)(4,1)S(1)} %compare_and_fusion.5, bf16[8,32,128,128]{3,2,1,0:T(8,128)(2,1)} %get-tuple-element.250, s32[]{:T(128)} %get-tuple-element.239), kind=kOutput, calls=%fused_computation.24.clone.1 | convolution fusion | flops 270532608 | bytes 7340704 | tf_op jit(solution)/shard_map/while/body/eval_jaxpr/tij,tjf->tif/dot_general | solution.py:26
  232.9 6.5 %scatter_fusion.1 = f32[8,128,256]{2,1,0:T(8,128)S(1)} fusion(f32[8,128,256]{2,1,0:T(8,128)S(1)} %get-tuple-element.240, s32[32]{0:T(128)S(1)} %get-tuple-element.205, f32[32,128,256]{2,1,0:T(8,128)} %convolution_multiply_fusion.5), kind=kCustom, calls=%fused_computation.3.clone.1 | custom fusion | flops 1048576 | bytes 12583040 | tf_op jit(solution)/shard_map/while/body/eval_jaxpr/scatter-add | solution.py:27
  241.7 3.9 %convolution_multiply_fusion.5 = f32[32,128,256]{2,1,0:T(8,128)} fusion(f32[32]{0:T(128)S(1)} %fusion.53, bf16[32,128,256]{2,1,0:T(8,128)(2,1)S(1)} %gather_fusion.1, pred[32]{0:T(512)(128)(4,1)S(1)} %compare_and_fusion.5, bf16[8,32,128,128]{3,2,1,0:T(8,128)(2,1)} %get-tuple-element.250, s32[]{:T(128)} %get-tuple-element.239), kind=kOutput, calls=%fused_computation.24.clone.1 | convolution fusion | flops 270532608 | bytes 7340704 | tf_op jit(solution)/shard_map/while/body/eval_jaxpr/tij,tjf->tif/dot_general | solution.py:26
  245.6 6.4 %scatter_fusion.1 = f32[8,128,256]{2,1,0:T(8,128)S(1)} fusion(f32[8,128,256]{2,1,0:T(8,128)S(1)} %get-tuple-element.240, s32[32]{0:T(128)S(1)} %get-tuple-element.205, f32[32,128,256]{2,1,0:T(8,128)} %convolution_multiply_fusion.5), kind=kCustom, calls=%fused_computation.3.clone.1 | custom fusion | flops 1048576 | bytes 12583040 | tf_op jit(solution)/shard_map/while/body/eval_jaxpr/scatter-add | solution.py:27
  254.4 3.9 %convolution_multiply_fusion.5 = f32[32,128,256]{2,1,0:T(8,128)} fusion(f32[32]{0:T(128)S(1)} %fusion.53, bf16[32,128,256]{2,1,0:T(8,128)(2,1)S(1)} %gather_fusion.1, pred[32]{0:T(512)(128)(4,1)S(1)} %compare_and_fusion.5, bf16[8,32,128,128]{3,2,1,0:T(8,128)(2,1)} %get-tuple-element.250, s32[]{:T(128)} %get-tuple-element.239), kind=kOutput, calls=%fused_computation.24.clone.1 | convolution fusion | flops 270532608 | bytes 7340704 | tf_op jit(solution)/shard_map/while/body/eval_jaxpr/tij,tjf->tif/dot_general | solution.py:26
  258.4 6.4 %scatter_fusion.1 = f32[8,128,256]{2,1,0:T(8,128)S(1)} fusion(f32[8,128,256]{2,1,0:T(8,128)S(1)} %get-tuple-element.240, s32[32]{0:T(128)S(1)} %get-tuple-element.205, f32[32,128,256]{2,1,0:T(8,128)} %convolution_multiply_fusion.5), kind=kCustom, calls=%fused_computation.3.clone.1 | custom fusion | flops 1048576 | bytes 12583040 | tf_op jit(solution)/shard_map/while/body/eval_jaxpr/scatter-add | solution.py:27
  267.2 3.9 %convolution_multiply_fusion.5 = f32[32,128,256]{2,1,0:T(8,128)} fusion(f32[32]{0:T(128)S(1)} %fusion.53, bf16[32,128,256]{2,1,0:T(8,128)(2,1)S(1)} %gather_fusion.1, pred[32]{0:T(512)(128)(4,1)S(1)} %compare_and_fusion.5, bf16[8,32,128,128]{3,2,1,0:T(8,128)(2,1)} %get-tuple-element.250, s32[]{:T(128)} %get-tuple-element.239), kind=kOutput, calls=%fused_computation.24.clone.1 | convolution fusion | flops 270532608 | bytes 7340704 | tf_op jit(solution)/shard_map/while/body/eval_jaxpr/tij,tjf->tif/dot_general | solution.py:26
  271.1 6.5 %scatter_fusion.1 = f32[8,128,256]{2,1,0:T(8,128)S(1)} fusion(f32[8,128,256]{2,1,0:T(8,128)S(1)} %get-tuple-element.240, s32[32]{0:T(128)S(1)} %get-tuple-element.205, f32[32,128,256]{2,1,0:T(8,128)} %convolution_multiply_fusion.5), kind=kCustom, calls=%fused_computation.3.clone.1 | custom fusion | flops 1048576 | bytes 12583040 | tf_op jit(solution)/shard_map/while/body/eval_jaxpr/scatter-add | solution.py:27
  279.9 3.9 %convolution_multiply_fusion.5 = f32[32,128,256]{2,1,0:T(8,128)} fusion(f32[32]{0:T(128)S(1)} %fusion.53, bf16[32,128,256]{2,1,0:T(8,128)(2,1)S(1)} %gather_fusion.1, pred[32]{0:T(512)(128)(4,1)S(1)} %compare_and_fusion.5, bf16[8,32,128,128]{3,2,1,0:T(8,128)(2,1)} %get-tuple-element.250, s32[]{:T(128)} %get-tuple-element.239), kind=kOutput, calls=%fused_computation.24.clone.1 | convolution fusion | flops 270532608 | bytes 7340704 | tf_op jit(solution)/shard_map/while/body/eval_jaxpr/tij,tjf->tif/dot_general | solution.py:26
  283.9 6.5 %scatter_fusion.1 = f32[8,128,256]{2,1,0:T(8,128)S(1)} fusion(f32[8,128,256]{2,1,0:T(8,128)S(1)} %get-tuple-element.240, s32[32]{0:T(128)S(1)} %get-tuple-element.205, f32[32,128,256]{2,1,0:T(8,128)} %convolution_multiply_fusion.5), kind=kCustom, calls=%fused_computation.3.clone.1 | custom fusion | flops 1048576 | bytes 12583040 | tf_op jit(solution)/shard_map/while/body/eval_jaxpr/scatter-add | solution.py:27
  292.9 23.6 %reduce-scatter.5.cloned.1.call-done = bf16[4,128,256]{2,1,0:T(8,128)(2,1)} async-done(((bf16[16,128,256]{2,1,0:T(8,128)(2,1)}), bf16[4,128,256]{2,1,0:T(8,128)(2,1)}) %reduce-scatter.5.cloned.1.call-update) | async-done | bytes 262160 | tf_op jit(solution)/shard_map/reduce_scatter | solution.py:72
  (122 shorter events, 65.7 us)
Async XLA Ops:
  6.5 309.9 %copy-start = (bf16[256,256]{1,0:T(8,128)(2,1)S(1)}, bf16[256,256]{1,0:T(8,128)(2,1)}, u32[]{:S(2)}) copy-start(bf16[256,256]{1,0:T(8,128)(2,1)} %param.22) | copy-start | bytes 393220
  6.5 45.8 %all-gather.3.cloned.1.call-start = ((), (), s32[]{:S(2)}) async-start(), calls=%async_computation.2 | async-start | bytes 1179648 | tf_op jit(solution)/shard_map/all_gather | solution.py:82
  7.3 129.3 %reduce-scatter.3.cloned.1.call-start = ((), (), s32[]{:S(2)}) async-start(), calls=%async_computation.3 | async-start | bytes 655360 | tf_op jit(solution)/shard_map/reduce_scatter | solution.py:72
  114.4 22.2 %copy-start.1 = (bf16[128,256]{1,0:T(8,128)(2,1)S(1)}, bf16[128,256]{1,0:T(8,128)(2,1)}, u32[]{:S(2)}) copy-start(bf16[128,256]{1,0:T(8,128)(2,1)} %param.20) | copy-start | bytes 196612
  114.4 22.1 %copy-start.2 = (f32[256]{0:T(256)S(1)}, f32[256]{0:T(256)}, u32[]{:S(2)}) copy-start(f32[256]{0:T(256)} %param.21) | copy-start | bytes 3076
  116.0 72.2 %all-gather.5.cloned.1.call-start = ((), (), s32[]{:S(2)}) async-start(), calls=%async_computation.4 | async-start | bytes 2359296 | tf_op jit(solution)/shard_map/all_gather | solution.py:91
  138.4 178.1 %reduce-scatter.5.cloned.1.call-start = ((), (), s32[]{:S(2)}) async-start(), calls=%async_computation.5 | async-start | bytes 1310720 | tf_op jit(solution)/shard_map/reduce_scatter | solution.py:72
  291.7 24.8 %copy-start.3 = (f32[256]{0:T(256)S(1)}, f32[256]{0:T(256)}, u32[]{:S(2)}) copy-start(f32[256]{0:T(256)} %param.23) | copy-start | bytes 3076
Sparse Core Ops, SparseCore 0:
  9.5 42.8 all-gather.2
  116.1 20.4 reduce-scatter.2
  138.9 49.2 all-gather.4
  293.0 23.4 reduce-scatter.4
where the time goes:
time: 327 us; the launch traced here: 325 us
  waiting for transfers between devices  134 us (41%)
  other arithmetic  77.7 us (24%)
  matrix products  53.4 us (16%)
  local copies, waits for them, and re-layouts  45.6 us (14%)
  between operations  13.2 us (4%)
    scatter-add x16, other arithmetic, advance(): return (totals.at[slot_set].add(products * alive_set[:, None, None]), None)  72.9 us
    all_gather x1, waiting for transfers between devices, body(): sources = lax.all_gather(hidden, 'member', axis=0, tiled=True)  49.8 us
    dot_general x16, matrix products, advance(): jnp.einsum('tij,tjf->tif', tile_set, source, preferred_element_type=jnp.f...  47.9 us
    reduce_scatter x2, waiting for transfers between devices, reduce_rows(): lax.psum_scatter(spread_sums.reshape(group_count * block_count, tile_size...  44.1 us
    gather x16, local copies, waits for them, and re-layouts, advance(): source = jnp.take(sources, column_set, axis=0)  41.7 us
    all_gather x1, waiting for transfers between devices, body(): gathered = lax.all_gather(local_rows, 'member', axis=0, tiled=True)  39.3 us
  transfers between devices with their start and end apart: 4, of which 4 were waited for; matrix products, arithmetic and copies ran while one was open for 2% of the time, Pallas kernels for 0%

commit v1 on v0

--- a/solution.py
+++ b/solution.py
@@ -79,7 +79,14 @@
         ).astype(jnp.float32)
 
     local_rows = features.reshape(block_count, tile_size, features.shape[1])
-    gathered = lax.all_gather(local_rows, "member", axis=0, tiled=True)
+    ring = [local_rows]
+    for hop in range(7):
+        ring.append(lax.ppermute(ring[-1], "member", [(dev, (dev + 1) % 8) for dev in range(8)]))
+    gathered = jnp.roll(
+        jnp.concatenate(ring[::-1], axis=0),
+        (lax.axis_index("member") + 1) * ring[0].shape[0],
+        axis=0,
+    )
     first_sum = reduce_rows(
         fold_tiles(gathered, edge_tiles, slot_ids, column_ids, alive_mask, slot_total)
     ).astype(jnp.bfloat16)

time: 327 us -> 339 us (1.037)
  waiting for transfers between devices: 134 us -> 141 us
    ppermute x0 -> x7, waiting for transfers between devices: none -> 48.3 us  [body(): lax.ppermute(ring[-1], 'member', [(dev, (dev + 1) % 8) for dev in range(8)])]
    all_gather x1 -> x0, waiting for transfers between devices: 39.3 us -> none  [body(): gathered = lax.all_gather(local_rows, 'member', axis=0, tiled=True)]
  transfers between devices with their start and end apart: 4 -> 10, of which waited for: 4 -> 10; matrix products, arithmetic and copies ran while one was open for 2% -> 2% of each run, Pallas kernels for 0% -> 0%
where the time goes in v1:
time: 339 us; the launch traced here: 337 us
  waiting for transfers between devices  141 us (42%)
  other arithmetic  77.5 us (23%)
  matrix products  53.5 us (16%)
  local copies, waits for them, and re-layouts  47.6 us (14%)
  between operations  13.3 us (4%)
    scatter-add x16, other arithmetic, advance(): return (totals.at[slot_set].add(products * alive_set[:, None, None]), None)  72.9 us
    all_gather x1, waiting for transfers between devices, body(): sources = lax.all_gather(hidden, 'member', axis=0, tiled=True)  49.8 us
    ppermute x7, waiting for transfers between devices, body(): lax.ppermute(ring[-1], 'member', [(dev, (dev + 1) % 8) for dev in range(8)])  48.3 us
    dot_general x16, matrix products, advance(): jnp.einsum('tij,tjf->tif', tile_set, source, preferred_element_type=jnp.f...  48 us
    reduce_scatter x2, waiting for transfers between devices, reduce_rows(): lax.psum_scatter(spread_sums.reshape(group_count * block_count, tile_size...  42.9 us
    gather x16, local copies, waits for them, and re-layouts, advance(): source = jnp.take(sources, column_set, axis=0)  41.5 us
  transfers between devices with their start and end apart: 10, of which 10 were waited for; matrix products, arithmetic and copies ran while one was open for 2% of the time, Pallas kernels for 0%

profile of v1, /device:TPU:0, one launch (start us, length us, event | category | flops | bytes accessed | tf_op | source)
XLA Modules:
  0.0 337.0 jit_solution(12486095950152931035)
XLA Ops:
  6.5 2.9 collective-permute-start
  9.5 6.8 %collective-permute-done = bf16[4,128,128]{2,1,0:T(8,128)(2,1)S(1)} collective-permute-done((bf16[4,128,128]{2,1,0:T(8,128)(2,1)}, bf16[4,128,128]{2,1,0:T(8,128)(2,1)S(1)}, u32[]{:S(2)}, u32[]{:S(2)}) %collective-permute-start) | collective-permute-done | bytes 131104 | tf_op jit(solution)/shard_map/ppermute | solution.py:84
  16.3 7.7 %collective-permute-done.1 = bf16[4,128,128]{2,1,0:T(8,128)(2,1)S(1)} collective-permute-done((bf16[4,128,128]{2,1,0:T(8,128)(2,1)S(1)}, bf16[4,128,128]{2,1,0:T(8,128)(2,1)S(1)}, u32[]{:S(2)}, u32[]{:S(2)}) %collective-permute-start.1) | collective-permute-done | bytes 131104 | tf_op jit(solution)/shard_map/ppermute | solution.py:84
  23.9 7.7 %collective-permute-done.2 = bf16[4,128,128]{2,1,0:T(8,128)(2,1)S(1)} collective-permute-done((bf16[4,128,128]{2,1,0:T(8,128)(2,1)S(1)}, bf16[4,128,128]{2,1,0:T(8,128)(2,1)S(1)}, u32[]{:S(2)}, u32[]{:S(2)}) %collective-permute-start.2) | collective-permute-done | bytes 131104 | tf_op jit(solution)/shard_map/ppermute | solution.py:84
  31.6 7.7 %collective-permute-done.3 = bf16[4,128,128]{2,1,0:T(8,128)(2,1)S(1)} collective-permute-done((bf16[4,128,128]{2,1,0:T(8,128)(2,1)S(1)}, bf16[4,128,128]{2,1,0:T(8,128)(2,1)S(1)}, u32[]{:S(2)}, u32[]{:S(2)}) %collective-permute-start.3) | collective-permute-done | bytes 131104 | tf_op jit(solution)/shard_map/ppermute | solution.py:84
  39.3 7.7 %collective-permute-done.4 = bf16[4,128,128]{2,1,0:T(8,128)(2,1)S(1)} collective-permute-done((bf16[4,128,128]{2,1,0:T(8,128)(2,1)S(1)}, bf16[4,128,128]{2,1,0:T(8,128)(2,1)S(1)}, u32[]{:S(2)}, u32[]{:S(2)}) %collective-permute-start.4) | collective-permute-done | bytes 131104 | tf_op jit(solution)/shard_map/ppermute | solution.py:84
  52.5 3.2 collective-permute-done.5
  55.7 7.7 %collective-permute-done.6 = bf16[4,128,128]{2,1,0:T(8,128)(2,1)S(1)} collective-permute-done((bf16[4,128,128]{2,1,0:T(8,128)(2,1)S(1)}, bf16[4,128,128]{2,1,0:T(8,128)(2,1)S(1)}, u32[]{:S(2)}, u32[]{:S(2)}) %collective-permute-start.6) | collective-permute-done | bytes 131104 | tf_op jit(solution)/shard_map/ppermute | solution.py:84
  65.8 61.8 %while.20 = (s32[]{:T(128)}, f32[8,128,128]{2,1,0:T(8,128)S(1)}, s32[8,32]{1,0:T(8,128)S(1)}, bf16[8,32,128,128]{3,2,1,0:T(8,128)(2,1)}, s32[8,32]{1,0:T(8,128)S...) while((s32[]{:T(128)}, f32[8,128,128]{2,1,0:T(8,128)S(1)}, s32[8,32]{1,0:T(8,128)S(1)}, ...), condition=%wide.region_3.4_spmd, body=%wide.region_1.3_spmd.sunk | while | flops 135792000 | bytes 12589089 | solution.py:30
  65.8 2.9 gather_fusion
  73.6 2.9 gather_fusion
  81.3 2.9 gather_fusion
  129.2 19.4 %reduce-scatter.3.cloned.1.call-done = bf16[4,128,128]{2,1,0:T(8,128)(2,1)} async-done(((bf16[16,128,128]{2,1,0:T(8,128)(2,1)}), bf16[4,128,128]{2,1,0:T(8,128)(2,1)}) %reduce-scatter.3.cloned.1.call-update) | async-done | bytes 131088 | tf_op jit(solution)/shard_map/reduce_scatter | solution.py:72
  150.5 49.8 %all-gather.2.cloned.1.call-done = bf16[32,128,256]{2,1,0:T(8,128)(2,1)} async-done(((bf16[4,128,256]{2,1,0:T(8,128)(2,1)}), bf16[32,128,256]{2,1,0:T(8,128)(2,1)}) %all-gather.2.cloned.1.call-update) | async-done | bytes 2097168 | tf_op jit(solution)/shard_map/all_gather | solution.py:98
  200.4 102.2 %while.21 = (s32[]{:T(128)}, f32[8,128,256]{2,1,0:T(8,128)S(1)}, s32[8,32]{1,0:T(8,128)S(1)}, bf16[8,32,128,128]{3,2,1,0:T(8,128)(2,1)}, s32[8,32]{1,0:T(8,128)S...) while((s32[]{:T(128)}, f32[8,128,256]{2,1,0:T(8,128)S(1)}, s32[8,32]{1,0:T(8,128)S(1)}, ...), condition=%wide.region_7.8_spmd, body=%wide.region_5.7_spmd.sunk | while | flops 271582592 | bytes 24123424 | solution.py:30
  202.7 3.9 %convolution_multiply_fusion.5 = f32[32,128,256]{2,1,0:T(8,128)} fusion(f32[32]{0:T(128)S(1)} %fusion.53, bf16[32,128,256]{2,1,0:T(8,128)(2,1)S(1)} %gather_fusion.1, pred[32]{0:T(512)(128)(4,1)S(1)} %compare_and_fusion.5, bf16[8,32,128,128]{3,2,1,0:T(8,128)(2,1)} %get-tuple-element.250, s32[]{:T(128)} %get-tuple-element.239), kind=kOutput, calls=%fused_computation.24.clone.1 | convolution fusion | flops 270532608 | bytes 7340704 | tf_op jit(solution)/shard_map/while/body/eval_jaxpr/tij,tjf->tif/dot_general | solution.py:26
  206.7 6.4 %scatter_fusion.1 = f32[8,128,256]{2,1,0:T(8,128)S(1)} fusion(f32[8,128,256]{2,1,0:T(8,128)S(1)} %get-tuple-element.240, s32[32]{0:T(128)S(1)} %get-tuple-element.205, f32[32,128,256]{2,1,0:T(8,128)} %convolution_multiply_fusion.5), kind=kCustom, calls=%fused_computation.3.clone.1 | custom fusion | flops 1048576 | bytes 12583040 | tf_op jit(solution)/shard_map/while/body/eval_jaxpr/scatter-add | solution.py:27
  215.5 3.9 %convolution_multiply_fusion.5 = f32[32,128,256]{2,1,0:T(8,128)} fusion(f32[32]{0:T(128)S(1)} %fusion.53, bf16[32,128,256]{2,1,0:T(8,128)(2,1)S(1)} %gather_fusion.1, pred[32]{0:T(512)(128)(4,1)S(1)} %compare_and_fusion.5, bf16[8,32,128,128]{3,2,1,0:T(8,128)(2,1)} %get-tuple-element.250, s32[]{:T(128)} %get-tuple-element.239), kind=kOutput, calls=%fused_computation.24.clone.1 | convolution fusion | flops 270532608 | bytes 7340704 | tf_op jit(solution)/shard_map/while/body/eval_jaxpr/tij,tjf->tif/dot_general | solution.py:26
  219.4 6.4 %scatter_fusion.1 = f32[8,128,256]{2,1,0:T(8,128)S(1)} fusion(f32[8,128,256]{2,1,0:T(8,128)S(1)} %get-tuple-element.240, s32[32]{0:T(128)S(1)} %get-tuple-element.205, f32[32,128,256]{2,1,0:T(8,128)} %convolution_multiply_fusion.5), kind=kCustom, calls=%fused_computation.3.clone.1 | custom fusion | flops 1048576 | bytes 12583040 | tf_op jit(solution)/shard_map/while/body/eval_jaxpr/scatter-add | solution.py:27
  228.3 3.9 %convolution_multiply_fusion.5 = f32[32,128,256]{2,1,0:T(8,128)} fusion(f32[32]{0:T(128)S(1)} %fusion.53, bf16[32,128,256]{2,1,0:T(8,128)(2,1)S(1)} %gather_fusion.1, pred[32]{0:T(512)(128)(4,1)S(1)} %compare_and_fusion.5, bf16[8,32,128,128]{3,2,1,0:T(8,128)(2,1)} %get-tuple-element.250, s32[]{:T(128)} %get-tuple-element.239), kind=kOutput, calls=%fused_computation.24.clone.1 | convolution fusion | flops 270532608 | bytes 7340704 | tf_op jit(solution)/shard_map/while/body/eval_jaxpr/tij,tjf->tif/dot_general | solution.py:26
  232.2 6.5 %scatter_fusion.1 = f32[8,128,256]{2,1,0:T(8,128)S(1)} fusion(f32[8,128,256]{2,1,0:T(8,128)S(1)} %get-tuple-element.240, s32[32]{0:T(128)S(1)} %get-tuple-element.205, f32[32,128,256]{2,1,0:T(8,128)} %convolution_multiply_fusion.5), kind=kCustom, calls=%fused_computation.3.clone.1 | custom fusion | flops 1048576 | bytes 12583040 | tf_op jit(solution)/shard_map/while/body/eval_jaxpr/scatter-add | solution.py:27
  241.0 3.9 %convolution_multiply_fusion.5 = f32[32,128,256]{2,1,0:T(8,128)} fusion(f32[32]{0:T(128)S(1)} %fusion.53, bf16[32,128,256]{2,1,0:T(8,128)(2,1)S(1)} %gather_fusion.1, pred[32]{0:T(512)(128)(4,1)S(1)} %compare_and_fusion.5, bf16[8,32,128,128]{3,2,1,0:T(8,128)(2,1)} %get-tuple-element.250, s32[]{:T(128)} %get-tuple-element.239), kind=kOutput, calls=%fused_computation.24.clone.1 | convolution fusion | flops 270532608 | bytes 7340704 | tf_op jit(solution)/shard_map/while/body/eval_jaxpr/tij,tjf->tif/dot_general | solution.py:26
  245.0 6.5 %scatter_fusion.1 = f32[8,128,256]{2,1,0:T(8,128)S(1)} fusion(f32[8,128,256]{2,1,0:T(8,128)S(1)} %get-tuple-element.240, s32[32]{0:T(128)S(1)} %get-tuple-element.205, f32[32,128,256]{2,1,0:T(8,128)} %convolution_multiply_fusion.5), kind=kCustom, calls=%fused_computation.3.clone.1 | custom fusion | flops 1048576 | bytes 12583040 | tf_op jit(solution)/shard_map/while/body/eval_jaxpr/scatter-add | solution.py:27
  253.8 3.9 %convolution_multiply_fusion.5 = f32[32,128,256]{2,1,0:T(8,128)} fusion(f32[32]{0:T(128)S(1)} %fusion.53, bf16[32,128,256]{2,1,0:T(8,128)(2,1)S(1)} %gather_fusion.1, pred[32]{0:T(512)(128)(4,1)S(1)} %compare_and_fusion.5, bf16[8,32,128,128]{3,2,1,0:T(8,128)(2,1)} %get-tuple-element.250, s32[]{:T(128)} %get-tuple-element.239), kind=kOutput, calls=%fused_computation.24.clone.1 | convolution fusion | flops 270532608 | bytes 7340704 | tf_op jit(solution)/shard_map/while/body/eval_jaxpr/tij,tjf->tif/dot_general | solution.py:26
  257.8 6.4 %scatter_fusion.1 = f32[8,128,256]{2,1,0:T(8,128)S(1)} fusion(f32[8,128,256]{2,1,0:T(8,128)S(1)} %get-tuple-element.240, s32[32]{0:T(128)S(1)} %get-tuple-element.205, f32[32,128,256]{2,1,0:T(8,128)} %convolution_multiply_fusion.5), kind=kCustom, calls=%fused_computation.3.clone.1 | custom fusion | flops 1048576 | bytes 12583040 | tf_op jit(solution)/shard_map/while/body/eval_jaxpr/scatter-add | solution.py:27
  266.6 3.9 %convolution_multiply_fusion.5 = f32[32,128,256]{2,1,0:T(8,128)} fusion(f32[32]{0:T(128)S(1)} %fusion.53, bf16[32,128,256]{2,1,0:T(8,128)(2,1)S(1)} %gather_fusion.1, pred[32]{0:T(512)(128)(4,1)S(1)} %compare_and_fusion.5, bf16[8,32,128,128]{3,2,1,0:T(8,128)(2,1)} %get-tuple-element.250, s32[]{:T(128)} %get-tuple-element.239), kind=kOutput, calls=%fused_computation.24.clone.1 | convolution fusion | flops 270532608 | bytes 7340704 | tf_op jit(solution)/shard_map/while/body/eval_jaxpr/tij,tjf->tif/dot_general | solution.py:26
  270.5 6.4 %scatter_fusion.1 = f32[8,128,256]{2,1,0:T(8,128)S(1)} fusion(f32[8,128,256]{2,1,0:T(8,128)S(1)} %get-tuple-element.240, s32[32]{0:T(128)S(1)} %get-tuple-element.205, f32[32,128,256]{2,1,0:T(8,128)} %convolution_multiply_fusion.5), kind=kCustom, calls=%fused_computation.3.clone.1 | custom fusion | flops 1048576 | bytes 12583040 | tf_op jit(solution)/shard_map/while/body/eval_jaxpr/scatter-add | solution.py:27
  279.3 3.9 %convolution_multiply_fusion.5 = f32[32,128,256]{2,1,0:T(8,128)} fusion(f32[32]{0:T(128)S(1)} %fusion.53, bf16[32,128,256]{2,1,0:T(8,128)(2,1)S(1)} %gather_fusion.1, pred[32]{0:T(512)(128)(4,1)S(1)} %compare_and_fusion.5, bf16[8,32,128,128]{3,2,1,0:T(8,128)(2,1)} %get-tuple-element.250, s32[]{:T(128)} %get-tuple-element.239), kind=kOutput, calls=%fused_computation.24.clone.1 | convolution fusion | flops 270532608 | bytes 7340704 | tf_op jit(solution)/shard_map/while/body/eval_jaxpr/tij,tjf->tif/dot_general | solution.py:26
  283.3 6.5 %scatter_fusion.1 = f32[8,128,256]{2,1,0:T(8,128)S(1)} fusion(f32[8,128,256]{2,1,0:T(8,128)S(1)} %get-tuple-element.240, s32[32]{0:T(128)S(1)} %get-tuple-element.205, f32[32,128,256]{2,1,0:T(8,128)} %convolution_multiply_fusion.5), kind=kCustom, calls=%fused_computation.3.clone.1 | custom fusion | flops 1048576 | bytes 12583040 | tf_op jit(solution)/shard_map/while/body/eval_jaxpr/scatter-add | solution.py:27
  292.1 3.9 %convolution_multiply_fusion.5 = f32[32,128,256]{2,1,0:T(8,128)} fusion(f32[32]{0:T(128)S(1)} %fusion.53, bf16[32,128,256]{2,1,0:T(8,128)(2,1)S(1)} %gather_fusion.1, pred[32]{0:T(512)(128)(4,1)S(1)} %compare_and_fusion.5, bf16[8,32,128,128]{3,2,1,0:T(8,128)(2,1)} %get-tuple-element.250, s32[]{:T(128)} %get-tuple-element.239), kind=kOutput, calls=%fused_computation.24.clone.1 | convolution fusion | flops 270532608 | bytes 7340704 | tf_op jit(solution)/shard_map/while/body/eval_jaxpr/tij,tjf->tif/dot_general | solution.py:26
  296.1 6.5 %scatter_fusion.1 = f32[8,128,256]{2,1,0:T(8,128)S(1)} fusion(f32[8,128,256]{2,1,0:T(8,128)S(1)} %get-tuple-element.240, s32[32]{0:T(128)S(1)} %get-tuple-element.205, f32[32,128,256]{2,1,0:T(8,128)} %convolution_multiply_fusion.5), kind=kCustom, calls=%fused_computation.3.clone.1 | custom fusion | flops 1048576 | bytes 12583040 | tf_op jit(solution)/shard_map/while/body/eval_jaxpr/scatter-add | solution.py:27
  305.0 23.6 %reduce-scatter.5.cloned.1.call-done = bf16[4,128,256]{2,1,0:T(8,128)(2,1)} async-done(((bf16[16,128,256]{2,1,0:T(8,128)(2,1)}), bf16[4,128,256]{2,1,0:T(8,128)(2,1)}) %reduce-scatter.5.cloned.1.call-update) | async-done | bytes 262160 | tf_op jit(solution)/shard_map/reduce_scatter | solution.py:72
  (152 shorter events, 86.9 us)
Async XLA Ops:
  6.5 322.1 %copy-start = (bf16[256,256]{1,0:T(8,128)(2,1)S(1)}, bf16[256,256]{1,0:T(8,128)(2,1)}, u32[]{:S(2)}) copy-start(bf16[256,256]{1,0:T(8,128)(2,1)} %param.22) | copy-start | bytes 393220
  6.5 58.2 %copy-start.1 = (bf16[512,128]{1,0:T(8,128)(2,1)S(1)}, bf16[512,128]{1,0:T(8,128)(2,1)}, u32[]{:S(2)}) copy-start(bf16[512,128]{1,0:T(8,128)(2,1)} %param.14) | copy-start | bytes 393220
  6.5 142.1 %reduce-scatter.3.cloned.1.call-start = ((), (), s32[]{:S(2)}) async-start(), calls=%async_computation.2 | async-start | bytes 655360 | tf_op jit(solution)/shard_map/reduce_scatter | solution.py:72
  6.5 9.7 %collective-permute-start = (bf16[4,128,128]{2,1,0:T(8,128)(2,1)}, bf16[4,128,128]{2,1,0:T(8,128)(2,1)S(1)}, u32[]{:S(2)}, u32[]{:S(2)}) collective-permute-start(bf16[4,128,128]{2,1,0:T(8,128)(2,1)} %bitcast.86), channel_id=1, source_target_pairs={{0,1},{1,2},{2,3},{3,4},{4,5},{5,6},{6,7},{7,0},{8,9},{9,10},{10,1... | collective-permute-start | bytes 393224 | tf_op jit(solution)/shard_map/ppermute | solution.py:84
  16.3 7.7 %collective-permute-start.1 = (bf16[4,128,128]{2,1,0:T(8,128)(2,1)S(1)}, bf16[4,128,128]{2,1,0:T(8,128)(2,1)S(1)}, u32[]{:S(2)}, u32[]{:S(2)}) collective-permute-start(bf16[4,128,128]{2,1,0:T(8,128)(2,1)S(1)} %collective-permute-done), channel_id=1, source_target_pairs={{0,1},{1,2},{2,3},{3,4},{4,5},{5,6},{6,7},{7,0},{8,9},{9,10},{10,1... | collective-permute-start | bytes 393224 | tf_op jit(solution)/shard_map/ppermute | solution.py:84
  23.9 7.7 %collective-permute-start.2 = (bf16[4,128,128]{2,1,0:T(8,128)(2,1)S(1)}, bf16[4,128,128]{2,1,0:T(8,128)(2,1)S(1)}, u32[]{:S(2)}, u32[]{:S(2)}) collective-permute-start(bf16[4,128,128]{2,1,0:T(8,128)(2,1)S(1)} %collective-permute-done.1), channel_id=1, source_target_pairs={{0,1},{1,2},{2,3},{3,4},{4,5},{5,6},{6,7},{7,0},{8,9},{9,10},{10,1... | collective-permute-start | bytes 393224 | tf_op jit(solution)/shard_map/ppermute | solution.py:84
  31.6 7.7 %collective-permute-start.3 = (bf16[4,128,128]{2,1,0:T(8,128)(2,1)S(1)}, bf16[4,128,128]{2,1,0:T(8,128)(2,1)S(1)}, u32[]{:S(2)}, u32[]{:S(2)}) collective-permute-start(bf16[4,128,128]{2,1,0:T(8,128)(2,1)S(1)} %collective-permute-done.2), channel_id=1, source_target_pairs={{0,1},{1,2},{2,3},{3,4},{4,5},{5,6},{6,7},{7,0},{8,9},{9,10},{10,1... | collective-permute-start | bytes 393224 | tf_op jit(solution)/shard_map/ppermute | solution.py:84
  39.2 7.7 %collective-permute-start.4 = (bf16[4,128,128]{2,1,0:T(8,128)(2,1)S(1)}, bf16[4,128,128]{2,1,0:T(8,128)(2,1)S(1)}, u32[]{:S(2)}, u32[]{:S(2)}) collective-permute-start(bf16[4,128,128]{2,1,0:T(8,128)(2,1)S(1)} %collective-permute-done.3), channel_id=1, source_target_pairs={{0,1},{1,2},{2,3},{3,4},{4,5},{5,6},{6,7},{7,0},{8,9},{9,10},{10,1... | collective-permute-start | bytes 393224 | tf_op jit(solution)/shard_map/ppermute | solution.py:84
  46.9 8.8 %collective-permute-start.5 = (bf16[4,128,128]{2,1,0:T(8,128)(2,1)S(1)}, bf16[4,128,128]{2,1,0:T(8,128)(2,1)S(1)}, u32[]{:S(2)}, u32[]{:S(2)}) collective-permute-start(bf16[4,128,128]{2,1,0:T(8,128)(2,1)S(1)} %collective-permute-done.4), channel_id=1, source_target_pairs={{0,1},{1,2},{2,3},{3,4},{4,5},{5,6},{6,7},{7,0},{8,9},{9,10},{10,1... | collective-permute-start | bytes 393224 | tf_op jit(solution)/shard_map/ppermute | solution.py:84
  55.7 7.7 %collective-permute-start.6 = (bf16[4,128,128]{2,1,0:T(8,128)(2,1)S(1)}, bf16[4,128,128]{2,1,0:T(8,128)(2,1)S(1)}, u32[]{:S(2)}, u32[]{:S(2)}) collective-permute-start(bf16[4,128,128]{2,1,0:T(8,128)(2,1)S(1)} %collective-permute-done.5), channel_id=1, source_target_pairs={{0,1},{1,2},{2,3},{3,4},{4,5},{5,6},{6,7},{7,0},{8,9},{9,10},{10,1... | collective-permute-start | bytes 393224 | tf_op jit(solution)/shard_map/ppermute | solution.py:84
  127.6 21.0 %copy-start.2 = (bf16[128,256]{1,0:T(8,128)(2,1)S(1)}, bf16[128,256]{1,0:T(8,128)(2,1)}, u32[]{:S(2)}) copy-start(bf16[128,256]{1,0:T(8,128)(2,1)} %param.20) | copy-start | bytes 196612
  127.6 21.0 %copy-start.3 = (f32[256]{0:T(256)S(1)}, f32[256]{0:T(256)}, u32[]{:S(2)}) copy-start(f32[256]{0:T(256)} %param.21) | copy-start | bytes 3076
  129.2 71.1 %all-gather.2.cloned.1.call-start = ((), (), s32[]{:S(2)}) async-start(), calls=%async_computation.3 | async-start | bytes 2359296 | tf_op jit(solution)/shard_map/all_gather | solution.py:98
  150.4 178.2 %reduce-scatter.5.cloned.1.call-start = ((), (), s32[]{:S(2)}) async-start(), calls=%async_computation.4 | async-start | bytes 1310720 | tf_op jit(solution)/shard_map/reduce_scatter | solution.py:72
  303.8 24.8 %copy-start.4 = (f32[256]{0:T(256)S(1)}, f32[256]{0:T(256)}, u32[]{:S(2)}) copy-start(f32[256]{0:T(256)} %param.23) | copy-start | bytes 3076
Sparse Core Ops, SparseCore 0:
  129.3 19.2 reduce-scatter.2
  150.9 49.2 all-gather.1
  305.1 23.4 reduce-scatter.4
